TPU v7x, 128 devices: a whole 4x4x4 slice. The times are simulated.
128 devices in a mesh: sector: 4 (over y_hi, core), owner: 32 (over x, y_lo, z).
Axes of the slice: x: 4, y: 4 (y_hi: 2, y_lo: 2; y = y_hi * 2 + y_lo), z: 4, core: 2. Of those that a mesh axis runs over, the one named last changes fastest.
Arguments:
- broadcast_ops: float32 [4, 4, 1024, 1024], P('sector', None, 'owner'), may hold values from -0.1875 to 0.1875
- resident_ops: float32 [4, 32, 1024, 1024], P('sector', 'owner'), may hold values from -6 to 6
- integrals: float32 [4, 32, 4, 4], P('sector', 'owner'), may hold values from -3 to 3
- owner_list: int32 [32, 4], P('owner'), may hold values from 0 to 3, as said below
Outputs:
- complementary: float32 [4, 32, 2, 1024, 1024], P('sector', 'owner')
Inputs may be any that keep to these rules, and one draw needn't show every extreme that they name: `owner_list`: in each row one sector group is named exactly 2 times, one is not named, and every other is named once.
All inputs are finite; a program needn't handle non-finite values.
Results may differ from a plain program's by a relative error of at most 0.012.
Values may be sent and summed in bfloat16 or wider, within the bound.
A program may use at most 64 MiB of HBM per device.

v0:
```python
import jax
import jax.numpy as jnp
from jax import lax
from jax.sharding import PartitionSpec as P

CAP = 2


def shards(broadcast_ops, resident_ops, integrals, owner_list):
    highest = lax.Precision.HIGHEST
    shared = broadcast_ops[0]
    resident = resident_ops[0, 0]
    weights = integrals[0, 0]
    owners = owner_list[0]
    pair_count = owners.shape[0]
    slot_count = CAP
    sector_id = lax.axis_index("sector")
    products = jnp.einsum(
        "krj,jn->krn",
        lax.all_gather(shared.astype(jnp.bfloat16), "owner", axis=1, tiled=True).astype(
            jnp.float32
        ),
        resident,
        precision=highest,
    )
    pair_index = jnp.arange(pair_count)
    same_owner = owners[:, None] == owners[None, :]
    earlier = pair_index[:, None] < pair_index[None, :]
    slot_rank = jnp.sum((same_owner & earlier).astype(jnp.int32), axis=0)
    partial_ops = jnp.einsum("pk,kmn->pmn", weights, products, precision=highest)
    pair_total = lax.psum(partial_ops.astype(jnp.bfloat16), "sector").astype(jnp.float32)
    selector = (
        (owners[None, :] == sector_id) & (slot_rank[None, :] == jnp.arange(slot_count)[:, None])
    ).astype(jnp.float32)
    result = jnp.einsum("cp,pmn->cmn", selector, pair_total, precision=highest)
    return result[None, None]


def solution(mesh):
    in_specs = (
        P("sector", None, "owner", None),
        P("sector", "owner", None, None),
        P("sector", "owner", None, None),
        P("owner", None),
    )
    out_specs = P("sector", "owner", None, None, None)
    return jax.shard_map(shards, mesh=mesh, in_specs=in_specs, out_specs=out_specs, check_vma=False)
```

profile of v0, /device:TPU:1, one launch (start us, length us, event | category | flops | bytes accessed | tf_op | source)
XLA Modules:
  0.0 435.2 jit_solution(6021242355717869884)
XLA Ops:
  6.5 0.0 copy-start
  6.5 0.0 all-gather.3.cloned.1.call-start
  6.5 1.8 convert_element_type.19
  8.3 0.0 all-gather.3.cloned.1.call-update
  8.4 0.0 all-reduce.2.cloned.1.call-start
  8.4 149.4 %all-gather.3.cloned.1.call-done = bf16[1,4,1024,1024]{3,2,1,0:T(8,128)(2,1)} async-done(((bf16[1,4,32,1024]{3,2,1,0:T(8,128)(2,1)}), bf16[1,4,1024,1024]{3,2,1,0:T(8,128)(2,1)}) %all-gather.3.cloned.1.call-update) | async-done | bytes 8388624 | tf_op jit(solution)/shard_map/all_gather | solution.py:20
  157.8 31.4 %fusion.2 = f32[4,1024,1024]{2,1,0:T(8,128)S(1)} fusion(bf16[1,4,1024,1024]{3,2,1,0:T(8,128)(2,1)} %all-gather.3.cloned.1.call-done, f32[1,1,1024,1024]{3,2,1,0:T(8,128)} %param.5), kind=kOutput, calls=%fused_computation.2 | convolution fusion | flops 51539607552 | bytes 29360128 | tf_op jit(solution)/shard_map/krj,jn->krn/dot_general | solution.py:18
  189.2 0.0 copy-done
  189.2 44.7 %convert_bitcast_fusion = bf16[4,1024,1024]{2,0,1:T(4,128)(2,1)} fusion(f32[4,1024,1024]{2,1,0:T(8,128)S(1)} %fusion.2, f32[1,1,4,4]{3,2,1,0:T(4,128)S(1)} %copy-done), kind=kOutput, calls=%fused_computation.4 | convolution fusion | flops 205520896 | bytes 25165888 | tf_op jit(solution)/shard_map/pk,kmn->pmn/dot_general | solution.py:30
  233.9 0.0 copy-start.1
  233.9 0.0 all-reduce.2.cloned.1.call-update
  233.9 0.6 copy-done.1
  234.6 0.1 convert_reduce_fusion
  234.7 180.7 %all-reduce.2.cloned.1.call-done = bf16[4,1024,1024]{2,0,1:T(4,128)(2,1)} async-done(((bf16[4,1024,1024]{2,0,1:T(4,128)(2,1)}), bf16[4,1024,1024]{2,0,1:T(4,128)(2,1)}) %all-reduce.2.cloned.1.call-update) | async-done | bytes 8388624 | tf_op jit(solution)/shard_map/psum | solution.py:31
  415.4 7.0 %convolution_bitcast_fusion = f32[1,1,2,1024,1024]{4,2,3,1,0:T(2,128)S(1)} fusion(bf16[4,1024,1024]{2,0,1:T(4,128)(2,1)} %all-reduce.2.cloned.1.call-done, pred[4]{0:T(512)(128)(4,1)S(1)} %compare_bitcast_fusion, s32[4]{0:T(128)S(1)} %convert_reduce_fusion), kind=kOutput, calls=%fused_computation.5 | convolution fusion | flops 16777232 | bytes 16777236 | tf_op jit(solution)/shard_map/cp,pmn->cmn/dot_general | solution.py:35
  422.4 6.0 %copy.6 = f32[1,1,2,1024,1024]{4,3,2,1,0:T(8,128)} copy(f32[1,1,2,1024,1024]{4,2,3,1,0:T(2,128)S(1)} %convolution_bitcast_fusion) | data formatting | bytes 16777216 | tf_op jit(solution)/shard_map/broadcast_in_dim | solution.py:36
  (1 shorter events, 0.0 us)
Async XLA Ops:
  6.5 182.6 %copy-start = (f32[1,1,4,4]{3,2,1,0:T(4,128)S(1)}, f32[1,1,4,4]{3,2,1,0:T(4,128)}, u32[]{:S(2)}) copy-start(f32[1,1,4,4]{3,2,1,0:T(4,128)} %param.6) | copy-start | bytes 196
  6.5 151.2 %all-gather.3.cloned.1.call-start = ((), (), s32[]{:S(2)}) async-start(), calls=%async_computation.1 | async-start | bytes 8650752 | tf_op jit(solution)/shard_map/all_gather | solution.py:20
  8.4 407.0 %all-reduce.2.cloned.1.call-start = ((), (), s32[]{:S(2)}) async-start(), calls=%async_computation | async-start | bytes 16777216 | tf_op jit(solution)/shard_map/psum | solution.py:31
  233.9 0.7 copy-start.1
Sparse Core Ops, SparseCore 0:
  9.0 148.7 all-gather.2
  234.1 181.2 all-reduce.1
where the time goes:
time: 435 us
  waiting for transfers between devices  330 us (76%)
  matrix products  83.2 us (19%)
  between operations  13.4 us (3%)
  local copies, waits for them, and re-layouts  6.59 us (2%)
    psum x1, waiting for transfers between devices, shards(): lax.psum(partial_ops.astype(jnp.bfloat16), 'sector').astype(jnp.float32)  181 us
    all_gather x1, waiting for transfers between devices, shards(): lax.all_gather(shared.astype(jnp.bfloat16), 'owner', axis=1, tiled=True)  149 us
    dot_general x1, matrix products, shards(): jnp.einsum('pk,kmn->pmn', weights, products, precision=highest)  44.7 us
    dot_general x1, matrix products, shards(): jnp.einsum('krj,jn->krn', lax.all_gather(shared.astype(jnp.bfloat16), 'ow...  31.4 us
  transfers between devices with their start and end apart: 2, of which 2 were waited for; matrix products, arithmetic and copies ran while one was open for 0% of the time, Pallas kernels for 0%

commit v1 on v0

--- a/solution.py
+++ b/solution.py
@@ -4,6 +4,11 @@
 from jax.sharding import PartitionSpec as P
 
 CAP = 2
+
+
+def swapped_in(array, axis, along):
+    stack = jnp.stack([array] * lax.axis_size(axis))
+    return jnp.concatenate(lax.all_to_all(stack, axis, 0, 0), axis=along)
 
 
 def shards(broadcast_ops, resident_ops, integrals, owner_list):
@@ -17,9 +22,7 @@
     sector_id = lax.axis_index("sector")
     products = jnp.einsum(
         "krj,jn->krn",
-        lax.all_gather(shared.astype(jnp.bfloat16), "owner", axis=1, tiled=True).astype(
-            jnp.float32
-        ),
+        swapped_in(shared.astype(jnp.bfloat16), "owner", 1).astype(jnp.float32),
         resident,
         precision=highest,
     )

time: 435 us -> 377 us (0.87)
  waiting for transfers between devices: 330 us -> 161 us
  blocking collectives: 0 us -> 103 us
  local copies, waits for them, and re-layouts: 6.59 us -> 16.4 us
    all_gather x1 -> x0, waiting for transfers between devices: 149 us -> none  [shards(): lax.all_gather(shared.astype(jnp.bfloat16), 'owner', axis=1, tiled=True)]
    all_to_all x0 -> x1, blocking collectives: none -> 103 us  [swapped_in(): return jnp.concatenate(lax.all_to_all(stack, axis, 0, 0), axis=along)]
    psum x1, waiting for transfers between devices: 181 us -> 160 us  [shards(): lax.psum(partial_ops.astype(jnp.bfloat16), 'sector').astype(jnp.float32)]
    all_to_all x0 -> x1, local copies, waits for them, and re-layouts: none -> 8.79 us  [swapped_in(): return jnp.concatenate(lax.all_to_all(stack, axis, 0, 0), axis=along)]
  transfers between devices with their start and end apart: 2 -> 1, of which waited for: 2 -> 1; matrix products, arithmetic and copies ran while one was open for 0% -> 0% of each run, Pallas kernels for 0% -> 0%
where the time goes in v1:
time: 377 us
  waiting for transfers between devices  161 us (43%)
  blocking collectives  103 us (27%)
  matrix products  81.9 us (22%)
  local copies, waits for them, and re-layouts  16.4 us (4%)
  between operations  13.4 us (4%)
    psum x1, waiting for transfers between devices, shards(): lax.psum(partial_ops.astype(jnp.bfloat16), 'sector').astype(jnp.float32)  160 us
    all_to_all x1, blocking collectives, swapped_in(): return jnp.concatenate(lax.all_to_all(stack, axis, 0, 0), axis=along)  103 us
    dot_general x1, matrix products, shards(): jnp.einsum('pk,kmn->pmn', weights, products, precision=highest)  44.7 us
    dot_general x1, matrix products, shards(): jnp.einsum('krj,jn->krn', swapped_in(shared.astype(jnp.bfloat16), 'owner'...  30.2 us
    all_to_all x1, local copies, waits for them, and re-layouts, swapped_in(): return jnp.concatenate(lax.all_to_all(stack, axis, 0, 0), axis=along)  8.79 us
  transfers between devices with their start and end apart: 1, of which 1 were waited for; matrix products, arithmetic and copies ran while one was open for 0% of the time, Pallas kernels for 0%

profile of v1, /device:TPU:1, one launch (start us, length us, event | category | flops | bytes accessed | tf_op | source)
XLA Modules:
  0.0 376.7 jit_solution(14369492109656285635)
XLA Ops:
  6.5 0.0 copy-start
  6.5 0.0 all-reduce.2.cloned.1.call-start
  6.5 1.1 convert_bitcast_fusion.1
  7.6 1.1 stack.5
  8.7 103.2 %all_to_all.5 = bf16[32,4,32,1024]{3,2,1,0:T(8,128)(2,1)} all-to-all(bf16[32,4,32,1024]{3,2,1,0:T(8,128)(2,1)S(1)} %stack.5), channel_id=1, replica_groups=mesh['sector'=4,'owner'=32] {'owner'}, dimensions={0} | all-to-all | bytes 16777216 | tf_op jit(solution)/shard_map/all_to_all | solution.py:11
  111.9 0.0 copy-start.1
  111.9 8.8 %copy.10 = bf16[32,4,32,1024]{3,2,0,1:T(8,128)(2,1)} copy(bf16[32,4,32,1024]{3,2,1,0:T(8,128)(2,1)} %all_to_all.5) | data formatting | bytes 16777216 | tf_op jit(solution)/shard_map/all_to_all | solution.py:11
  120.7 0.0 copy-done.1
  120.7 30.2 %fusion.4 = f32[4,1024,1024]{2,1,0:T(8,128)S(1)} fusion(bf16[4,1024,1024]{2,1,0:T(8,128)(2,1)} %bitcast.27, f32[1,1,1024,1024]{3,2,1,0:T(8,128)S(1)} %copy-done.1), kind=kOutput, calls=%fused_computation.4 | convolution fusion | flops 51539607552 | bytes 29360128 | tf_op jit(solution)/shard_map/krj,jn->krn/dot_general | solution.py:23
  150.9 0.0 copy-done
  150.9 44.7 %convert_bitcast_fusion = bf16[4,1024,1024]{2,0,1:T(4,128)(2,1)} fusion(f32[4,1024,1024]{2,1,0:T(8,128)S(1)} %fusion.4, f32[1,1,4,4]{3,2,1,0:T(4,128)S(1)} %copy-done), kind=kOutput, calls=%fused_computation.2 | convolution fusion | flops 205520896 | bytes 25165888 | tf_op jit(solution)/shard_map/pk,kmn->pmn/dot_general | solution.py:33
  195.7 0.0 copy-start.2
  195.7 0.0 all-reduce.2.cloned.1.call-update
  195.7 0.6 copy-done.2
  196.3 0.1 convert_reduce_fusion
  196.4 160.5 %all-reduce.2.cloned.1.call-done = bf16[4,1024,1024]{2,0,1:T(4,128)(2,1)} async-done(((bf16[4,1024,1024]{2,0,1:T(4,128)(2,1)}), bf16[4,1024,1024]{2,0,1:T(4,128)(2,1)}) %all-reduce.2.cloned.1.call-update) | async-done | bytes 8388624 | tf_op jit(solution)/shard_map/psum | solution.py:34
  356.9 7.0 %convolution_bitcast_fusion = f32[1,1,2,1024,1024]{4,2,3,1,0:T(2,128)S(1)} fusion(bf16[4,1024,1024]{2,0,1:T(4,128)(2,1)} %all-reduce.2.cloned.1.call-done, pred[4]{0:T(512)(128)(4,1)S(1)} %compare_bitcast_fusion, s32[4]{0:T(128)S(1)} %convert_reduce_fusion), kind=kOutput, calls=%fused_computation.3 | convolution fusion | flops 16777232 | bytes 16777236 | tf_op jit(solution)/shard_map/cp,pmn->cmn/dot_general | solution.py:38
  363.9 6.0 %copy.12 = f32[1,1,2,1024,1024]{4,3,2,1,0:T(8,128)} copy(f32[1,1,2,1024,1024]{4,2,3,1,0:T(2,128)S(1)} %convolution_bitcast_fusion) | data formatting | bytes 16777216 | tf_op jit(solution)/shard_map/broadcast_in_dim | solution.py:39
  (1 shorter events, 0.0 us)
Async XLA Ops:
  6.5 144.4 %copy-start = (f32[1,1,4,4]{3,2,1,0:T(4,128)S(1)}, f32[1,1,4,4]{3,2,1,0:T(4,128)}, u32[]{:S(2)}) copy-start(f32[1,1,4,4]{3,2,1,0:T(4,128)} %param.6) | copy-start | bytes 196
  6.5 350.4 %all-reduce.2.cloned.1.call-start = ((), (), s32[]{:S(2)}) async-start(), calls=%async_computation.1 | async-start | bytes 16777216 | tf_op jit(solution)/shard_map/psum | solution.py:34
  111.9 8.8 %copy-start.1 = (f32[1,1,1024,1024]{3,2,1,0:T(8,128)S(1)}, f32[1,1,1024,1024]{3,2,1,0:T(8,128)}, u32[]{:S(2)}) copy-start(f32[1,1,1024,1024]{3,2,1,0:T(8,128)} %param.5) | copy-start | bytes 12582916
  195.7 0.7 copy-start.2
Sparse Core Ops, SparseCore 0:
  195.8 161.0 all-reduce.1
